TPU v7x, 32 devices: a whole 2x2x4 slice. The times are simulated.
32 devices in a mesh: dp: 8 (over z, x), tensor: 4 (over y, core).
Axes of the slice: x: 2, y: 2, z: 4, core: 2. Of those that a mesh axis runs over, the one named last changes fastest.
Arguments:
- tokens: bfloat16 [48, 260, 768], P('dp'), may hold values from -6 to 6
- cotangent: bfloat16 [48, 260, 768], P('dp'), may hold values from -6 to 6
- split_point: int32 [48], P('dp'), may hold values from 0 to 32
- w_qkv: bfloat16 [3, 768, 768], P(None, None, 'tensor'), may hold values from -0.21875 to 0.21875
- w_out: bfloat16 [768, 768], P('tensor'), may hold values from -0.75 to 0.75
- w_up: bfloat16 [768, 3072], P(None, 'tensor'), may hold values from -0.21875 to 0.21875
- w_down: bfloat16 [3072, 768], P('tensor'), may hold values from -0.109375 to 0.109375
- gain_one: float32 [768], replicated, may hold values from 0.1 to 1.9
- shift_one: float32 [768], replicated, may hold values from -3 to 3
- gain_two: float32 [768], replicated, may hold values from 0.1 to 1.9
- shift_two: float32 [768], replicated, may hold values from -3 to 3
Outputs:
- output: bfloat16 [48, 260, 768], P('dp')
- grad_tokens: bfloat16 [48, 260, 768], P('dp')
- grad_qkv: float32 [3, 768, 768], P(None, 'dp', 'tensor')
- grad_out: float32 [768, 768], P('tensor', 'dp')
- grad_up: float32 [768, 3072], P('dp', 'tensor')
- grad_down: float32 [3072, 768], P('tensor', 'dp')
- grad_gain_one: float32 [768], P('dp')
- grad_shift_one: float32 [768], P('dp')
- grad_gain_two: float32 [768], P('dp')
- grad_shift_two: float32 [768], P('dp')
All inputs are finite; a program needn't handle non-finite values.
Results may differ from a plain program's by a relative error of at most 0.013.
Values sent between devices are 32-bit elements; how exact they have to be, the bound alone decides.
A program may use at most 128 MiB of HBM per device.

v0:
```python
from functools import partial
import jax
import jax.numpy as jnp
from jax import lax
from jax.sharding import PartitionSpec as P

HD = 64
PATCHES = 196
EPSILON = 1e-05


def layer_norm(values, gain_vec, shift_vec):
    row_mean = jnp.mean(values, axis=-1, keepdims=True)
    centered = values - row_mean
    variance = jnp.mean(centered * centered, axis=-1, keepdims=True)
    return centered * lax.rsqrt(variance + EPSILON) * gain_vec + shift_vec


def attention_forward(inputs, allowed, w_qkv, w_out, gain_one, shift_one):
    batch, length, width = inputs.shape
    local = w_qkv.shape[2]
    head_count = local // HD
    normed = layer_norm(inputs, gain_one, shift_one).astype(jnp.bfloat16)
    packed = jnp.einsum("btd,cde->cbte", normed, w_qkv, preferred_element_type=jnp.float32).astype(
        jnp.bfloat16
    )
    queries = packed[0].reshape(batch, length, head_count, HD)
    keys = packed[1].reshape(batch, length, head_count, HD)
    values = packed[2].reshape(batch, length, head_count, HD)
    scores = jnp.einsum(
        "bqhe,bkhe->bhqk", queries, keys, preferred_element_type=jnp.float32
    ) * HD ** (-0.5)
    scores = jnp.where(allowed[:, None], scores, -1e30)
    log_total = jax.nn.logsumexp(scores, axis=-1, keepdims=True)
    attn_probs = jnp.exp(scores - log_total)
    probs_low = attn_probs.astype(jnp.bfloat16)
    mixed = jnp.einsum("bhqk,bkhe->bqhe", probs_low, values, preferred_element_type=jnp.float32)
    mixed = mixed.reshape(batch, length, local).astype(jnp.bfloat16)
    partial_out = jnp.einsum("btk,kd->btd", mixed, w_out, preferred_element_type=jnp.float32)
    return (normed, queries, keys, values, attn_probs, probs_low, mixed, partial_out)


def mlp_forward(middle, w_up, gain_two, shift_two):
    normed_two = layer_norm(middle, gain_two, shift_two).astype(jnp.bfloat16)
    pre_act = jnp.einsum("btd,df->btf", normed_two, w_up, preferred_element_type=jnp.float32)
    activated = jax.nn.gelu(pre_act, approximate=False).astype(jnp.bfloat16)
    return (normed_two, pre_act, activated)


def per_device(
    tokens,
    cotangent,
    split_point,
    w_qkv,
    w_out,
    w_up,
    w_down,
    gain_one,
    shift_one,
    gain_two,
    shift_two,
):
    inputs = tokens.astype(jnp.float32)
    batch, length, width = tokens.shape
    local = w_qkv.shape[2]
    head_count = local // HD
    score_scale = HD ** (-0.5)
    places = jnp.arange(length, dtype=jnp.int32)
    limit = jnp.maximum(places[None, :, None], PATCHES + split_point[:, None, None] - 1)
    allowed = places[None, None, :] <= limit
    normed, queries, keys, values, attn_probs, probs_low, mixed, partial_out = attention_forward(
        inputs, allowed, w_qkv, w_out, gain_one, shift_one
    )
    middle = inputs + lax.psum(partial_out, "tensor")
    normed_two, pre_act, activated = mlp_forward(middle, w_up, gain_two, shift_two)
    branch = jnp.einsum("btf,fd->btd", activated, w_down, preferred_element_type=jnp.float32)
    output = (middle + lax.psum(branch, "tensor")).astype(jnp.bfloat16)
    normed, queries, keys, values, attn_probs, probs_low, mixed, partial_out = attention_forward(
        inputs, allowed, w_qkv, w_out, gain_one, shift_one
    )
    middle = inputs + lax.psum(partial_out, "tensor")
    normed_two, pre_act, activated = mlp_forward(middle, w_up, gain_two, shift_two)
    grad_output = cotangent.astype(jnp.float32)
    grad_act = jnp.einsum("btd,fd->btf", cotangent, w_down, preferred_element_type=jnp.float32)
    gelu_pull = jax.vjp(partial(jax.nn.gelu, approximate=False), pre_act)[1]
    grad_pre = gelu_pull(grad_act)[0].astype(jnp.bfloat16)
    grad_down_local = jnp.einsum(
        "btf,btd->fd", activated, cotangent, preferred_element_type=jnp.float32
    )
    grad_up_local = jnp.einsum(
        "btd,btf->df", normed_two, grad_pre, preferred_element_type=jnp.float32
    )
    grad_normed_two = lax.psum(
        jnp.einsum("btf,df->btd", grad_pre, w_up, preferred_element_type=jnp.float32), "tensor"
    )
    norm_two_pull = jax.vjp(layer_norm, middle, gain_two, shift_two)[1]
    grad_mid_norm, grad_gain_two, grad_shift_two = norm_two_pull(grad_normed_two)
    grad_middle = grad_output + grad_mid_norm
    grad_mid_low = grad_middle.astype(jnp.bfloat16)
    grad_out_local = jnp.einsum(
        "btk,btd->kd", mixed, grad_mid_low, preferred_element_type=jnp.float32
    )
    grad_mix = jnp.einsum("btd,kd->btk", grad_mid_low, w_out, preferred_element_type=jnp.float32)
    grad_mix = grad_mix.astype(jnp.bfloat16).reshape(batch, length, head_count, HD)
    grad_probs = jnp.einsum("bqhe,bkhe->bhqk", grad_mix, values, preferred_element_type=jnp.float32)
    row_terms = jnp.sum(attn_probs * grad_probs, axis=-1, keepdims=True)
    grad_scores = (attn_probs * (grad_probs - row_terms)).astype(jnp.bfloat16)
    grad_query = (
        jnp.einsum("bhqk,bkhe->bqhe", grad_scores, keys, preferred_element_type=jnp.float32)
        * score_scale
    )
    grad_key = (
        jnp.einsum("bhqk,bqhe->bkhe", grad_scores, queries, preferred_element_type=jnp.float32)
        * score_scale
    )
    grad_value = jnp.einsum(
        "bhqk,bqhe->bkhe", probs_low, grad_mix, preferred_element_type=jnp.float32
    )
    grad_packed = (
        jnp.stack([grad_query, grad_key, grad_value])
        .reshape(3, batch, length, local)
        .astype(jnp.bfloat16)
    )
    grad_qkv_local = jnp.einsum(
        "btd,cbte->cde", normed, grad_packed, preferred_element_type=jnp.float32
    )
    grad_normed = lax.psum(
        jnp.einsum("cbte,cde->btd", grad_packed, w_qkv, preferred_element_type=jnp.float32),
        "tensor",
    )
    norm_one_pull = jax.vjp(layer_norm, inputs, gain_one, shift_one)[1]
    grad_in_norm, grad_gain_one, grad_shift_one = norm_one_pull(grad_normed)
    grad_tokens = (grad_middle + grad_in_norm).astype(jnp.bfloat16)
    (
        qkv_part,
        out_part,
        up_part,
        down_part,
        gain_one_part,
        shift_one_part,
        gain_two_part,
        shift_two_part,
    ) = (
        lax.psum_scatter(grad_qkv_local, "dp", scatter_dimension=1, tiled=True),
        lax.psum_scatter(grad_out_local, "dp", scatter_dimension=1, tiled=True),
        lax.psum_scatter(grad_up_local, "dp", scatter_dimension=0, tiled=True),
        lax.psum_scatter(grad_down_local, "dp", scatter_dimension=1, tiled=True),
        lax.psum_scatter(grad_gain_one, "dp", scatter_dimension=0, tiled=True),
        lax.psum_scatter(grad_shift_one, "dp", scatter_dimension=0, tiled=True),
        lax.psum_scatter(grad_gain_two, "dp", scatter_dimension=0, tiled=True),
        lax.psum_scatter(grad_shift_two, "dp", scatter_dimension=0, tiled=True),
    )
    return (
        output,
        grad_tokens,
        qkv_part,
        out_part,
        up_part,
        down_part,
        gain_one_part,
        shift_one_part,
        gain_two_part,
        shift_two_part,
    )


def solution(mesh):
    in_specs = (
        P("dp", None, None),
        P("dp", None, None),
        P("dp"),
        P(None, None, "tensor"),
        P("tensor", None),
        P(None, "tensor"),
        P("tensor", None),
        P(),
        P(),
        P(),
        P(),
    )
    out_specs = (
        P("dp", None, None),
        P("dp", None, None),
        P(None, "dp", "tensor"),
        P("tensor", "dp"),
        P("dp", "tensor"),
        P("tensor", "dp"),
        P("dp"),
        P("dp"),
        P("dp"),
        P("dp"),
    )
    return jax.shard_map(
        per_device, mesh=mesh, in_specs=in_specs, out_specs=out_specs, check_vma=False
    )
```

profile of v0, /device:TPU:0, one launch (start us, length us, event | category | flops | bytes accessed | tf_op | source)
XLA Modules:
  0.0 753.6 jit_solution(12247592497835204554)
XLA Ops:
  7.3 0.8 broadcast_add_fusion
  8.2 2.3 convert_reduce_fusion
  10.4 2.6 fusion.10
  13.4 2.8 convert_bitcast_fusion
  16.3 1.3 fusion.48
  17.6 1.6 copy.57
  19.2 2.3 copy.56
  21.4 1.4 copy.55
  22.8 2.9 fusion.4
  25.7 1.7 exponential_reduce_fusion
  27.5 2.3 convolution_convert_fusion.1
  29.8 0.9 copy-done.18
  30.7 3.0 fusion.36
  34.0 99.2 %all-reduce.10.cloned.1.call-done = f32[6,260,768]{2,1,0:T(8,128)} async-done(((f32[6,260,768]{2,1,0:T(8,128)}), f32[6,260,768]{2,1,0:T(8,128)}) %all-reduce.10.cloned.1.call-update) | async-done | bytes 4792336 | tf_op jit(solution)/shard_map/psum | solution.py:74
  133.2 3.7 fusion.47
  137.0 0.7 multiply_reduce_fusion.3
  137.8 3.8 fusion.23
  141.5 11.6 %multiply_convert_fusion.1 = (bf16[6,260,768]{2,1,0:T(8,128)(2,1)}, f32[6,260,768]{2,1,0:T(8,128)S(1)}) fusion(f32[6,260,768]{2,1,0:T(8,128)S(1)} %get-tuple-element.66, u8[260,768]{1,0:T(8,128)(4,1)S(1)} %get-tuple-element.48, u8[260,768]{1,0:T(8,128)(4,1)S(1)} %get-tuple-element.47), kind=kLoop, calls=%fused_computation.35 | loop fusion | flops 83865600 | bytes 12380160 | tf_op jit(solution)/shard_map/convert_element_type | solution.py:46
  153.2 3.4 add_convert_fusion.1
  156.6 1.4 copy-done.34
  158.0 4.3 fusion.27
  162.6 96.5 %all-reduce.12.cloned.1.call-done = f32[6,260,768]{2,1,0:T(8,128)} async-done(((f32[6,260,768]{2,1,0:T(8,128)}), f32[6,260,768]{2,1,0:T(8,128)}) %all-reduce.12.cloned.1.call-update) | async-done | bytes 4792336 | tf_op jit(solution)/shard_map/psum | solution.py:93
  259.1 4.9 multiply_reduce_fusion.1
  264.4 3.6 fusion.45
  268.0 0.6 fusion.19
  268.6 1.5 copy-done.7
  270.2 1.4 copy-done.17
  271.6 2.4 convolution_bitcast_fusion.4
  274.0 2.5 convolution_convert_fusion.2
  276.5 1.3 copy.60
  277.8 6.5 convolution_convert_fusion
  284.3 6.8 multiply_reduce_fusion
  291.5 6.3 multiply_convert_fusion
  297.8 1.8 copy-done.6
  299.6 1.9 multiply_convert_fusion.3
  301.5 2.3 copy.66
  303.8 2.2 copy.64
  306.0 3.6 multiply_convert_fusion.2
  310.1 5.0 convolution_bitcast_fusion.3
  315.1 2.8 copy.77
  317.9 4.7 reshape.158
  322.7 6.1 fusion.25
  328.9 4.5 convolution_bitcast_fusion
  333.6 7.4 convolution_bitcast_fusion.2
  341.1 6.2 convolution_bitcast_fusion.1
  347.4 0.6 dynamic-slice
  348.6 5.2 reduce-scatter.15.cloned.1.call-done
  353.8 1.6 copy.80
  355.5 68.6 %reduce-scatter.13.cloned.1.call-done = f32[96,576]{1,0:T(8,128)} async-done(((f32[768,576]{1,0:T(8,128)}), f32[96,576]{1,0:T(8,128)}) %reduce-scatter.13.cloned.1.call-update) | async-done | bytes 221200
  424.0 1.1 reshape.159
  425.1 0.8 copy.68
  425.9 174.9 %all-reduce.14.cloned.1.call-done = (f32[6,260,768]{2,1,0:T(8,128)}, f32[6,260,768]{2,1,0:T(8,128)}) async-done(((f32[6,260,768]{2,1,0:T(8,128)}, f32[6,260,768]{2,1,0:T(8,128)}), (f32[6,260,768]{2,1,0:T(8,128)}, f32[6,260,768]{2,1,0:T(8,128)})) %all-reduce.14.cloned.1.call-update) | async-done | bytes 9584656 | tf_op jit(solution)/shard_map/psum | solution.py:77
  600.8 4.6 fusion.44
  605.4 3.9 fusion.9
  609.2 37.2 %all-reduce.4 = (f32[768]{0:T(1024)S(1)}, f32[768]{0:T(1024)S(1)}, f32[768]{0:T(1024)S(1)}, f32[768]{0:T(1024)S(1)}) all-reduce(f32[768]{0:T(1024)S(1)} %get-tuple-element.42, f32[768]{0:T(1024)S(1)} %get-tuple-element.45, f32[768]{0:T(1024)S(1)} %get-tuple-element.40, ...), channel_id=6, replica_groups=mesh['dp'=8,'tensor'=4] {'dp'}, use_global_device_ids=true, to_apply=%region_20.21.clone | all-reduce | flops 3072 | bytes 24576
  646.4 0.6 dynamic-slice.1
  647.0 0.6 dynamic-slice.3
  647.6 0.6 dynamic-slice.5
  648.2 0.6 dynamic-slice.7
  648.8 6.0 add_convert_fusion.2
  655.3 1.6 copy-done.9
  656.9 5.0 add_convert_fusion
  661.9 12.3 %reduce-scatter.9.cloned.1.call-done = f32[96,768]{1,0:T(8,128)} async-done(((f32[768,768]{1,0:T(8,128)}), f32[96,768]{1,0:T(8,128)}) %reduce-scatter.9.cloned.1.call-update) | async-done | bytes 294928 | tf_op jit(solution)/shard_map/reduce_scatter | solution.py:146
  674.2 72.4 %reduce-scatter.11.cloned.1.call-done = f32[768,96]{0,1:T(8,128)} async-done(((f32[768,768]{0,1:T(8,128)}), f32[768,96]{0,1:T(8,128)}) %reduce-scatter.11.cloned.1.call-update) | async-done | bytes 294928 | tf_op jit(solution)/shard_map/reduce_scatter | solution.py:147
  (96 shorter events, 3.4 us)
Async XLA Ops:
  7.2 130.5 %copy-start = (bf16[768,768]{1,0:T(8,128)(2,1)S(1)}, bf16[768,768]{1,0:T(8,128)(2,1)}, u32[]{:S(2)}) copy-start(bf16[768,768]{1,0:T(8,128)(2,1)} %param.16) | copy-start | bytes 3538948
  7.2 6.2 copy-start.25
  7.2 6.2 copy-start.31
  7.2 6.2 copy-start.29
  7.2 126.0 %all-reduce.10.cloned.1.call-start = ((), (), s32[]{:S(2)}) async-start(), calls=%async_computation.4 | async-start | bytes 9732096 | tf_op jit(solution)/shard_map/psum | solution.py:74
  7.3 6.1 copy-start.4
  25.7 4.1 copy-start.3
  25.7 1.8 copy-start.14
  27.5 3.2 copy-start.24
  29.8 0.9 copy-start.18
  33.8 225.3 %all-reduce.12.cloned.1.call-start = ((), (), s32[]{:S(2)}) async-start(), calls=%async_computation.5 | async-start | bytes 9732096 | tf_op jit(solution)/shard_map/psum | solution.py:93
  137.0 4.6 copy-start.2
  137.0 0.8 copy-start.26
  137.0 0.8 copy-start.32
  141.5 11.7 %copy-start.11 = (bf16[6,260,768]{2,1,0:T(8,128)(2,1)S(1)}, bf16[6,260,768]{2,1,0:T(8,128)(2,1)}, u32[]{:S(2)}) copy-start(bf16[6,260,768]{2,1,0:T(8,128)(2,1)} %param.12) | copy-start | bytes 7188484
  141.5 11.6 %copy-start.27 = (bf16[768,768]{1,0:T(8,128)(2,1)S(1)}, bf16[768,768]{1,0:T(8,128)(2,1)}, u32[]{:S(2)}) copy-start(bf16[768,768]{1,0:T(8,128)(2,1)} %param.17) | copy-start | bytes 3538948
  156.6 1.4 copy-start.34
  162.3 191.5 %reduce-scatter.15.cloned.1.call-start = ((), (), s32[]{:S(2)}) async-start(), calls=%async_computation.9 | async-start | bytes 884736
  259.1 5.2 copy-start.10
  264.4 3.6 copy-start.12
  268.0 2.2 copy-start.7
  268.0 3.6 copy-start.19
  270.2 1.4 copy-start.17
  277.8 6.5 copy-start.15
  277.8 6.5 copy-start.16
  291.1 132.9 %reduce-scatter.13.cloned.1.call-start = ((), (), s32[]{:S(2)}) async-start(), calls=%async_computation.8 | async-start | bytes 2211840
  297.8 1.8 copy-start.6
  299.6 6.4 copy-start.13
  310.1 5.0 copy-start.22
  317.9 4.8 copy-start.28
  322.6 278.1 %all-reduce.14.cloned.1.call-start = ((), (), s32[]{:S(2)}) async-start(), calls=%async_computation.10 | async-start | bytes 19464192 | tf_op jit(solution)/shard_map/psum | solution.py:77
  322.7 6.1 copy-start.20
  322.7 6.1 copy-start.21
  322.7 6.1 copy-start.23
  322.7 6.1 copy-start.30
  333.4 340.8 %reduce-scatter.9.cloned.1.call-start = ((), (), s32[]{:S(2)}) async-start(), calls=%async_computation.6 | async-start | bytes 2654208 | tf_op jit(solution)/shard_map/reduce_scatter | solution.py:146
  341.1 6.3 copy-start.33
  341.1 405.4 %reduce-scatter.11.cloned.1.call-start = ((), (), s32[]{:S(2)}) async-start(), calls=%async_computation.7 | async-start | bytes 2654208 | tf_op jit(solution)/shard_map/reduce_scatter | solution.py:147
  600.8 4.6 copy-start.8
  605.4 49.4 %slice-start = ((s8[4866048]{0:T(1024)(128)(4,1)}), s8[671744]{0:T(1024)(128)(4,1)S(1)}, s32[]{:S(2)}) async-start(s8[4866048]{0:T(1024)(128)(4,1)} %bitcast.87), calls=%async_computation.11 | async-start | bytes 1343488
  648.8 6.0 copy-start.5
  648.8 6.5 slice-start.1
  648.8 8.1 %copy-start.9 = (f32[6,260,768]{2,1,0:T(8,128)S(1)}, f32[6,260,768]{2,1,0:T(8,128)}, u32[]{:S(2)}) copy-start(f32[6,260,768]{2,1,0:T(8,128)} %get-tuple-element.54) | copy-start | bytes 14376964
  648.8 97.8 %copy-start.1 = (bf16[768,768]{1,0:T(8,128)(2,1)S(1)}, bf16[768,768]{1,0:T(8,128)(2,1)}, u32[]{:S(2)}) copy-start(bf16[768,768]{1,0:T(8,128)(2,1)} %param.16) | copy-start | bytes 3538948
Sparse Core Ops, SparseCore 0:
  33.9 99.2 all-reduce.9
  162.5 96.6 all-reduce.11
  291.2 62.5 reduce-scatter.14
  358.1 65.8 reduce-scatter.12
  426.5 174.2 all-reduce.13
  605.1 69.0 reduce-scatter.8
  678.6 67.8 reduce-scatter.10
where the time goes:
time: 762 us; the launch traced here: 754 us
  waiting for transfers between devices  529 us (69%)
  matrix products  75.3 us (10%)
  other arithmetic  58.8 us (8%)
  blocking collectives  37.2 us (5%)
  local copies, waits for them, and re-layouts  36.4 us (5%)
  between operations  15.5 us (2%)
    psum x1, waiting for transfers between devices, per_device(): output = (middle + lax.psum(branch, 'tensor')).astype(jnp.bfloat16)  175 us
    psum x1, waiting for transfers between devices, per_device(): middle = inputs + lax.psum(partial_out, 'tensor')  99.2 us
    psum x1, waiting for transfers between devices, per_device(): lax.psum(jnp.einsum('btf,df->btd', grad_pre, w_up, preferred_element_type...  96.5 us
    unnamed x9, waiting for transfers between devices  73.9 us
    reduce_scatter x1, waiting for transfers between devices, per_device(): lax.psum_scatter(grad_down_local, 'dp', scatter_dimension=1, tiled=True)  72.4 us
    unnamed x1, blocking collectives  37.2 us
    unnamed x84, local copies, waits for them, and re-layouts  23.5 us
  transfers between devices with their start and end apart: 7, of which 7 were waited for; matrix products, arithmetic and copies ran while one was open for 11% of the time, Pallas kernels for 0%

commit v1 on v0

--- a/solution.py
+++ b/solution.py
@@ -90,8 +90,11 @@
     grad_up_local = jnp.einsum(
         "btd,btf->df", normed_two, grad_pre, preferred_element_type=jnp.float32
     )
-    grad_normed_two = lax.psum(
-        jnp.einsum("btf,df->btd", grad_pre, w_up, preferred_element_type=jnp.float32), "tensor"
+    grad_normed_two = jnp.sum(
+        lax.all_gather(
+            jnp.einsum("btf,df->btd", grad_pre, w_up, preferred_element_type=jnp.float32), "tensor"
+        ),
+        axis=0,
     )
     norm_two_pull = jax.vjp(layer_norm, middle, gain_two, shift_two)[1]
     grad_mid_norm, grad_gain_two, grad_shift_two = norm_two_pull(grad_normed_two)

time: 762 us -> 798 us (1.047)
  waiting for transfers between devices: 529 us -> 547 us
  other arithmetic: 58.8 us -> 76.2 us
    all_gather x0 -> x1, waiting for transfers between devices: none -> 123 us  [per_device(): lax.all_gather(jnp.einsum('btf,df->btd', grad_pre, w_up, preferred_elemen...]
    psum x1 -> x0, waiting for transfers between devices: 96.5 us -> none  [per_device(): lax.psum(jnp.einsum('btf,df->btd', grad_pre, w_up, preferred_element_type...]
    reduce_sum x0 -> x1, other arithmetic: none -> 9.89 us  [per_device(): jnp.sum(lax.all_gather(jnp.einsum('btf,df->btd', grad_pre, w_up, preferre...]
    unnamed x9, waiting for transfers between devices: 73.9 us -> 65.5 us
    reduce_sum x3 -> x4, other arithmetic: 13.4 us -> 20.9 us  [layer_norm(): return centered * lax.rsqrt(variance + EPSILON) * gain_vec + shift_vec]
  transfers between devices with their start and end apart: 7 -> 7, of which waited for: 7 -> 6; matrix products, arithmetic and copies ran while one was open for 11% -> 11% of each run, Pallas kernels for 0% -> 0%
where the time goes in v1:
time: 798 us; the launch traced here: 789 us
  waiting for transfers between devices  547 us (69%)
  other arithmetic  76.2 us (10%)
  matrix products  75.4 us (9%)
  blocking collectives  37.3 us (5%)
  local copies, waits for them, and re-layouts  36.5 us (5%)
  between operations  15.5 us (2%)
    psum x1, waiting for transfers between devices, per_device(): output = (middle + lax.psum(branch, 'tensor')).astype(jnp.bfloat16)  175 us
    all_gather x1, waiting for transfers between devices, per_device(): lax.all_gather(jnp.einsum('btf,df->btd', grad_pre, w_up, preferred_elemen...  123 us
    psum x1, waiting for transfers between devices, per_device(): middle = inputs + lax.psum(partial_out, 'tensor')  99.2 us
    reduce_scatter x1, waiting for transfers between devices, per_device(): lax.psum_scatter(grad_down_local, 'dp', scatter_dimension=1, tiled=True)  72.3 us
    unnamed x9, waiting for transfers between devices  65.5 us
    unnamed x1, blocking collectives  37.3 us
    unnamed x84, local copies, waits for them, and re-layouts  23.8 us
    reduce_sum x4, other arithmetic, layer_norm(): return centered * lax.rsqrt(variance + EPSILON) * gain_vec + shift_vec  20.9 us
  transfers between devices with their start and end apart: 7, of which 6 were waited for; matrix products, arithmetic and copies ran while one was open for 11% of the time, Pallas kernels for 0%

profile of v1, /device:TPU:0, one launch (start us, length us, event | category | flops | bytes accessed | tf_op | source)
XLA Modules:
  0.0 789.4 jit_solution(2074817578457741909)
XLA Ops:
  7.3 0.8 broadcast_add_fusion
  8.2 2.3 convert_reduce_fusion
  10.4 2.6 fusion.10
  13.4 2.8 convert_bitcast_fusion
  16.3 1.3 fusion.48
  17.6 1.6 copy.57
  19.2 2.2 copy.56
  21.4 1.3 copy.55
  22.7 2.9 fusion.4
  25.6 1.7 exponential_reduce_fusion
  27.4 2.3 convolution_convert_fusion.1
  29.7 0.9 copy-done.18
  30.7 3.1 fusion.36
  34.0 99.2 %all-reduce.9.cloned.1.call-done = f32[6,260,768]{2,1,0:T(8,128)} async-done(((f32[6,260,768]{2,1,0:T(8,128)}), f32[6,260,768]{2,1,0:T(8,128)}) %all-reduce.9.cloned.1.call-update) | async-done | bytes 4792336 | tf_op jit(solution)/shard_map/psum | solution.py:74
  133.2 3.7 fusion.47
  137.0 0.7 multiply_reduce_fusion.3
  137.7 3.7 fusion.23
  141.5 11.6 %multiply_convert_fusion.1 = (bf16[6,260,768]{2,1,0:T(8,128)(2,1)}, f32[6,260,768]{2,1,0:T(8,128)S(1)}) fusion(f32[6,260,768]{2,1,0:T(8,128)S(1)} %get-tuple-element.65, u8[260,768]{1,0:T(8,128)(4,1)S(1)} %get-tuple-element.47, u8[260,768]{1,0:T(8,128)(4,1)S(1)} %get-tuple-element.46), kind=kLoop, calls=%fused_computation.35 | loop fusion | flops 83865600 | bytes 12380160 | tf_op jit(solution)/shard_map/convert_element_type | solution.py:46
  153.2 3.4 add_convert_fusion.1
  156.5 1.4 copy-done.34
  158.0 4.4 fusion.27
  162.7 123.2 %all-gather.3.cloned.1.call-done = f32[24,260,768]{2,1,0:T(8,128)} async-done(((f32[6,260,768]{2,1,0:T(8,128)}), f32[24,260,768]{2,1,0:T(8,128)}) %all-gather.3.cloned.1.call-update) | async-done | bytes 19169296 | tf_op jit(solution)/shard_map/all_gather | solution.py:94
  285.9 9.9 %reduce_sum.140 = f32[6,260,768]{2,1,0:T(8,128)} reduce(f32[4,6,260,768]{3,2,1,0:T(8,128)} %bitcast.88, f32[]{:T(128)} %constant.38.clone.1), dimensions={0}, to_apply=%region_8.9 | reduce | flops 3594240 | bytes 23961604 | tf_op jit(solution)/shard_map/reduce_sum | solution.py:93
  295.8 4.8 multiply_reduce_fusion.1
  301.0 3.6 fusion.45
  304.7 0.6 fusion.19
  305.3 1.5 copy-done.7
  306.8 1.4 copy-done.17
  308.2 2.4 convolution_bitcast_fusion.4
  310.6 2.5 convolution_convert_fusion.2
  313.1 1.3 copy.60
  314.4 6.5 convolution_convert_fusion
  320.9 6.7 multiply_reduce_fusion
  328.1 6.3 multiply_convert_fusion
  334.4 1.8 copy-done.6
  336.2 1.9 multiply_convert_fusion.3
  338.1 2.2 copy.66
  340.3 2.2 copy.64
  342.5 3.5 multiply_convert_fusion.2
  346.7 5.0 convolution_bitcast_fusion.3
  351.7 2.8 copy.77
  354.5 4.8 reshape.159
  359.4 6.1 fusion.25
  365.5 4.6 convolution_bitcast_fusion
  370.3 7.4 convolution_bitcast_fusion.2
  377.8 6.2 convolution_bitcast_fusion.1
  384.1 0.6 dynamic-slice
  385.4 7.6 reduce_sum.155
  393.0 1.6 copy.80
  394.6 65.3 %reduce-scatter.13.cloned.1.call-done = f32[96,576]{1,0:T(8,128)} async-done(((f32[768,576]{1,0:T(8,128)}), f32[96,576]{1,0:T(8,128)}) %reduce-scatter.13.cloned.1.call-update) | async-done | bytes 221200
  460.0 1.1 reshape.160
  461.1 0.8 copy.68
  461.9 175.1 %all-reduce.11.cloned.1.call-done = (f32[6,260,768]{2,1,0:T(8,128)}, f32[6,260,768]{2,1,0:T(8,128)}) async-done(((f32[6,260,768]{2,1,0:T(8,128)}, f32[6,260,768]{2,1,0:T(8,128)}), (f32[6,260,768]{2,1,0:T(8,128)}, f32[6,260,768]{2,1,0:T(8,128)})) %all-reduce.11.cloned.1.call-update) | async-done | bytes 9584656 | tf_op jit(solution)/shard_map/psum | solution.py:77
  636.9 4.6 fusion.44
  641.5 3.8 fusion.9
  645.4 37.3 %all-reduce.4 = (f32[768]{0:T(1024)S(1)}, f32[768]{0:T(1024)S(1)}, f32[768]{0:T(1024)S(1)}, f32[768]{0:T(1024)S(1)}) all-reduce(f32[768]{0:T(1024)S(1)} %get-tuple-element.42, f32[768]{0:T(1024)S(1)} %get-tuple-element.44, f32[768]{0:T(1024)S(1)} %get-tuple-element.40, ...), channel_id=7, replica_groups=mesh['dp'=8,'tensor'=4] {'dp'}, use_global_device_ids=true, to_apply=%region_20.21.clone | all-reduce | flops 3072 | bytes 24576
  682.7 0.6 dynamic-slice.1
  683.3 0.6 dynamic-slice.3
  683.9 0.6 dynamic-slice.5
  685.1 6.0 add_convert_fusion.2
  691.6 1.6 copy-done.9
  693.2 5.0 add_convert_fusion
  698.2 12.0 %reduce-scatter.9.cloned.1.call-done = f32[96,768]{1,0:T(8,128)} async-done(((f32[768,768]{1,0:T(8,128)}), f32[96,768]{1,0:T(8,128)}) %reduce-scatter.9.cloned.1.call-update) | async-done | bytes 294928 | tf_op jit(solution)/shard_map/reduce_scatter | solution.py:149
  710.1 72.3 %reduce-scatter.11.cloned.1.call-done = f32[768,96]{0,1:T(8,128)} async-done(((f32[768,768]{0,1:T(8,128)}), f32[768,96]{0,1:T(8,128)}) %reduce-scatter.11.cloned.1.call-update) | async-done | bytes 294928 | tf_op jit(solution)/shard_map/reduce_scatter | solution.py:150
  (98 shorter events, 4.1 us)
Async XLA Ops:
  7.2 130.5 %copy-start = (bf16[768,768]{1,0:T(8,128)(2,1)S(1)}, bf16[768,768]{1,0:T(8,128)(2,1)}, u32[]{:S(2)}) copy-start(bf16[768,768]{1,0:T(8,128)(2,1)} %param.16) | copy-start | bytes 3538948
  7.2 6.2 copy-start.25
  7.2 6.2 copy-start.31
  7.2 6.2 copy-start.29
  7.2 126.0 %all-reduce.9.cloned.1.call-start = ((), (), s32[]{:S(2)}) async-start(), calls=%async_computation.4 | async-start | bytes 9732096 | tf_op jit(solution)/shard_map/psum | solution.py:74
  7.3 6.1 copy-start.4
  25.6 4.1 copy-start.3
  25.6 1.8 copy-start.14
  27.4 3.2 copy-start.24
  29.7 0.9 copy-start.18
  33.8 252.1 %all-gather.3.cloned.1.call-start = ((), (), s32[]{:S(2)}) async-start(), calls=%async_computation.7 | async-start | bytes 24330240 | tf_op jit(solution)/shard_map/all_gather | solution.py:94
  136.9 4.5 copy-start.2
  136.9 0.8 copy-start.26
  137.0 0.8 copy-start.32
  141.5 11.7 %copy-start.11 = (bf16[6,260,768]{2,1,0:T(8,128)(2,1)S(1)}, bf16[6,260,768]{2,1,0:T(8,128)(2,1)}, u32[]{:S(2)}) copy-start(bf16[6,260,768]{2,1,0:T(8,128)(2,1)} %param.12) | copy-start | bytes 7188484
  141.5 11.6 %copy-start.27 = (bf16[768,768]{1,0:T(8,128)(2,1)S(1)}, bf16[768,768]{1,0:T(8,128)(2,1)}, u32[]{:S(2)}) copy-start(bf16[768,768]{1,0:T(8,128)(2,1)} %param.17) | copy-start | bytes 3538948
  156.5 1.5 copy-start.34
  162.4 230.6 %reduce-scatter.15.cloned.1.call-start = ((), (), s32[]{:S(2)}) async-start(), calls=%async_computation.9 | async-start | bytes 884736
  295.8 5.2 copy-start.10
  301.0 3.6 copy-start.12
  304.6 2.2 copy-start.7
  304.6 3.6 copy-start.19
  306.8 1.4 copy-start.17
  314.4 6.5 copy-start.15
  314.4 6.5 copy-start.16
  327.6 132.3 %reduce-scatter.13.cloned.1.call-start = ((), (), s32[]{:S(2)}) async-start(), calls=%async_computation.8 | async-start | bytes 2211840
  334.4 1.9 copy-start.6
  336.2 6.3 copy-start.13
  346.7 5.0 copy-start.22
  354.5 4.8 copy-start.28
  359.3 277.7 %all-reduce.11.cloned.1.call-start = ((), (), s32[]{:S(2)}) async-start(), calls=%async_computation.10 | async-start | bytes 19464192 | tf_op jit(solution)/shard_map/psum | solution.py:77
  359.3 6.2 copy-start.20
  359.3 6.2 copy-start.21
  359.3 6.2 copy-start.23
  359.4 6.1 copy-start.30
  370.1 340.0 %reduce-scatter.9.cloned.1.call-start = ((), (), s32[]{:S(2)}) async-start(), calls=%async_computation.5 | async-start | bytes 2654208 | tf_op jit(solution)/shard_map/reduce_scatter | solution.py:149
  377.8 6.3 copy-start.33
  377.8 404.6 %reduce-scatter.11.cloned.1.call-start = ((), (), s32[]{:S(2)}) async-start(), calls=%async_computation.6 | async-start | bytes 2654208 | tf_op jit(solution)/shard_map/reduce_scatter | solution.py:150
  636.9 4.6 copy-start.8
  641.5 49.5 %slice-start = ((s8[4866048]{0:T(1024)(128)(4,1)}), s8[671744]{0:T(1024)(128)(4,1)S(1)}, s32[]{:S(2)}) async-start(s8[4866048]{0:T(1024)(128)(4,1)} %bitcast.89), calls=%async_computation.11 | async-start | bytes 1343488
  685.1 6.0 copy-start.5
  685.1 6.5 slice-start.1
  685.1 8.1 %copy-start.9 = (f32[6,260,768]{2,1,0:T(8,128)S(1)}, f32[6,260,768]{2,1,0:T(8,128)}, u32[]{:S(2)}) copy-start(f32[6,260,768]{2,1,0:T(8,128)} %get-tuple-element.53) | copy-start | bytes 14376964
  685.1 97.3 %copy-start.1 = (bf16[768,768]{1,0:T(8,128)(2,1)S(1)}, bf16[768,768]{1,0:T(8,128)(2,1)}, u32[]{:S(2)}) copy-start(bf16[768,768]{1,0:T(8,128)(2,1)} %param.16) | copy-start | bytes 3538948
Sparse Core Ops, SparseCore 0:
  33.9 99.2 all-reduce.8
  162.5 123.3 all-gather.2
  327.7 62.4 reduce-scatter.14
  394.2 65.7 reduce-scatter.12
  462.6 174.2 all-reduce.10
  640.8 69.2 reduce-scatter.8
  714.2 68.1 reduce-scatter.10
